TPU v7x, 256 devices: a whole 4x4x8 slice. The times are simulated.
256 devices in a mesh: dp: 32 (over z, y), tensor: 8 (over x, core).
Axes of the slice: x: 4, y: 4, z: 8, core: 2. Of those that a mesh axis runs over, the one named last changes fastest.
Arguments:
- inputs: bfloat16 [16384, 4096], P('dp'), may hold values from -6 to 6
- weight: bfloat16 [4096, 4096], P(None, 'tensor'), may hold values from -0.09375 to 0.09375
- targets: bfloat16 [16384, 4096], P('dp', 'tensor'), may hold values from -6 to 6
- momentum: float32 [4096, 4096], P('dp', 'tensor'), may hold values from -6 to 6
Outputs:
- input_grad: bfloat16 [4096, 16384], P('tensor', 'dp')
- new_momentum: float32 [4096, 4096], P('dp', 'tensor')
- tree_norms: float32 [2], replicated
All inputs are finite; a program needn't handle non-finite values.
Results may differ from a plain program's by a relative error of at most 0.013.
Values may be sent and summed in bfloat16 or wider, within the bound.
A program may use at most 128 MiB of HBM per device.

v0:
```python
import math

import jax
import jax.numpy as jnp
from jax import lax
from jax.sharding import PartitionSpec as P

ROWS = 512


def partner(value, axis, stride):
    mask = 2**stride
    pairs = [(source, source ^ mask) for source in range(lax.axis_size(axis))]
    return lax.ppermute(value, axis, pairs)


def body(inputs, weight, targets, momentum):
    outputs = jnp.dot(inputs, weight, preferred_element_type=jnp.float32)
    error = (outputs - targets.astype(jnp.float32)).astype(jnp.bfloat16)
    summed = lax.psum_scatter(
        lax.dot_general(
            weight, error, (((1,), (1,)), ((), ())), preferred_element_type=jnp.float32
        ).astype(jnp.bfloat16),
        "tensor",
        scatter_dimension=0,
        tiled=True,
    )
    grad = lax.dot_general(
        inputs, error, (((0,), (0,)), ((), ())), preferred_element_type=jnp.float32
    )
    grad = grad * (1.0 / math.sqrt(ROWS))
    groups = lax.axis_size("dp")
    depth = groups.bit_length() - 1
    my_index = lax.axis_index("dp")
    block_rows = grad.shape[0] // groups
    columns = grad.shape[1]
    piece = grad.reshape(groups, block_rows, columns)
    last_sums = None
    for level in range(depth):
        my_bit = my_index >> level & 1
        paired = piece.reshape(piece.shape[0] // 2, 2, block_rows, columns)
        lower_half = paired[:, 0]
        upper_half = paired[:, 1]
        is_lower = my_bit == 0
        kept = jnp.where(is_lower, lower_half, upper_half)
        sent = jnp.where(is_lower, upper_half, lower_half)
        received = partner(sent, "dp", level)
        first = jnp.where(is_lower, kept, received)
        second = jnp.where(is_lower, received, kept)
        partials = jnp.stack(
            [jnp.sum(first * second), jnp.sum(first * first), jnp.sum(second * second)]
        )
        count_groups = groups >> level + 1
        my_group = my_index >> level + 1
        onehot = (jnp.arange(count_groups, dtype=jnp.int32) == my_group).astype(jnp.float32)
        table = onehot[:, None] * partials[None, :]
        totals = lax.psum(table, ("dp", "tensor"))
        sums = jnp.sum(onehot[:, None] * totals, axis=0)
        cross = sums[0]
        piece = (1.0 - cross / (2.0 * sums[1])) * first + (1.0 - cross / (2.0 * sums[2])) * second
        last_sums = sums
    combined = piece.reshape(block_rows, columns)
    width_total = weight.shape[0]
    tree_norms = jnp.sqrt(last_sums[1:3]) / width_total
    return (summed, 0.9 * momentum + combined, tree_norms)


def solution(mesh):
    return jax.shard_map(
        body,
        mesh=mesh,
        in_specs=(P("dp", None), P(None, "tensor"), P("dp", "tensor"), P("dp", "tensor")),
        out_specs=(P("tensor", "dp"), P("dp", "tensor"), P()),
        check_vma=False,
    )
```

profile of v0, /device:TPU:1, one launch (start us, length us, event | category | flops | bytes accessed | tf_op | source)
XLA Modules:
  0.0 719.7 jit_solution(9255067585885786011)
XLA Ops:
  7.2 6.0 fusion.2
  13.2 5.6 multiply_bitcast_fusion
  18.9 11.7 %reshape_reshape.3 = f32[16,2,128,512]{2,1,0,3:T(2,128)} reshape(f32[4096,512]{0,1:T(8,128)} %multiply_bitcast_fusion) | data formatting | bytes 16777216 | tf_op jit(solution)/shard_map/reshape;reshape | solution.py:41
  30.6 12.1 %fusion.5 = (f32[16,1,128,512]{2,1,0,3:T(1,128)}, f32[16,1,128,512]{2,1,0,3:T(1,128)}) fusion(f32[16,2,128,512]{2,1,0,3:T(2,128)} %reshape_reshape.3), kind=kLoop, calls=%fused_computation.67 | loop fusion | bytes 16777216 | tf_op jit(solution)/shard_map/slice | solution.py:42
  42.7 10.9 %copy.76 = f32[16,1,128,512]{3,2,0,1:T(8,128)} copy(f32[16,1,128,512]{2,1,0,3:T(1,128)} %get-tuple-element.43) | data formatting | bytes 8388608
  53.6 10.9 %copy.77 = f32[16,1,128,512]{3,2,0,1:T(8,128)} copy(f32[16,1,128,512]{2,1,0,3:T(1,128)} %get-tuple-element.44) | data formatting | bytes 8388608
  64.5 5.3 select_bitcast_fusion
  71.9 89.4 %collective-permute-done = f32[16,128,512]{2,1,0:T(8,128)} collective-permute-done((f32[16,128,512]{2,1,0:T(8,128)}, f32[16,128,512]{2,1,0:T(8,128)}, u32[]{:S(2)}, u32[]{:S(2)}) %collective-permute-start) | collective-permute-done | bytes 4194336 | tf_op jit(solution)/shard_map/ppermute | solution.py:14
  161.4 7.0 multiply_reduce_fusion.2
  170.4 81.5 %psum.35 = f32[16,3]{0,1:T(4,128)S(1)} all-reduce(f32[16,3]{0,1:T(4,128)S(1)} %broadcast_multiply_fusion.2), channel_id=1, replica_groups=mesh['dp'=32,'tensor'=8] {'dp','tensor'}, use_global_device_ids=true, to_apply=%region_4.5 | all-reduce | flops 48 | bytes 384 | tf_op jit(solution)/shard_map/psum | solution.py:57
  255.3 4.5 multiply_add_fusion
  263.8 4.3 fusion
  268.1 42.7 %collective-permute-done.1 = f32[8,128,512]{2,1,0:T(8,128)} collective-permute-done((f32[8,128,512]{2,1,0:T(8,128)S(1)}, f32[8,128,512]{2,1,0:T(8,128)}, u32[]{:S(2)}, u32[]{:S(2)}) %collective-permute-start.1) | collective-permute-done | bytes 2097184 | tf_op jit(solution)/shard_map/ppermute | solution.py:14
  310.8 6.5 multiply_reduce_fusion.5
  319.4 73.2 %psum.36 = f32[8,3]{0,1:T(4,128)S(1)} all-reduce(f32[8,3]{0,1:T(4,128)S(1)} %broadcast_multiply_fusion.1), channel_id=1, replica_groups=mesh['dp'=32,'tensor'=8] {'dp','tensor'}, use_global_device_ids=true, to_apply=%region_9.10 | all-reduce | flops 24 | bytes 192 | tf_op jit(solution)/shard_map/psum | solution.py:57
  395.9 2.8 multiply_add_fusion.1
  400.9 23.0 %collective-permute-done.2 = f32[4,128,512]{2,1,0:T(8,128)} collective-permute-done((f32[4,128,512]{2,1,0:T(8,128)S(1)}, f32[4,128,512]{2,1,0:T(8,128)}, u32[]{:S(2)}, u32[]{:S(2)}) %collective-permute-start.2) | collective-permute-done | bytes 1048608 | tf_op jit(solution)/shard_map/ppermute | solution.py:14
  423.8 3.1 multiply_reduce_fusion.8
  429.1 73.5 %psum.37 = f32[4,3]{1,0:T(4,128)S(1)} all-reduce(f32[4,3]{1,0:T(4,128)S(1)} %broadcast_multiply_fusion), channel_id=1, replica_groups=mesh['dp'=32,'tensor'=8] {'dp','tensor'}, use_global_device_ids=true, to_apply=%region_14.15 | all-reduce | flops 12 | bytes 96 | tf_op jit(solution)/shard_map/psum | solution.py:57
  507.5 25.0 %collective-permute-done.3 = f32[2,128,512]{2,1,0:T(8,128)S(1)} collective-permute-done((f32[2,128,512]{2,1,0:T(8,128)S(1)}, f32[2,128,512]{2,1,0:T(8,128)S(1)}, u32[]{:S(2)}, u32[]{:S(2)}) %collective-permute-start.3) | collective-permute-done | bytes 524320 | tf_op jit(solution)/shard_map/ppermute | solution.py:14
  535.5 73.3 %psum.38 = f32[2,3]{1,0:T(2,128)S(1)} all-reduce(f32[2,3]{1,0:T(2,128)S(1)} %broadcast_multiply_fusion.3), channel_id=1, replica_groups=mesh['dp'=32,'tensor'=8] {'dp','tensor'}, use_global_device_ids=true, to_apply=%region_19.20 | all-reduce | flops 6 | bytes 48 | tf_op jit(solution)/shard_map/psum | solution.py:57
  612.2 2.8 collective-permute-start.4
  615.0 14.4 %collective-permute-done.4 = f32[1,128,512]{2,1,0:T(8,128)S(1)} collective-permute-done((f32[1,128,512]{2,1,0:T(8,128)S(1)}, f32[1,128,512]{2,1,0:T(8,128)S(1)}, u32[]{:S(2)}, u32[]{:S(2)}) %collective-permute-start.4) | collective-permute-done | bytes 262176 | tf_op jit(solution)/shard_map/ppermute | solution.py:14
  632.2 74.0 %psum.39 = f32[1,3]{1,0:T(1,128)S(1)} all-reduce(f32[1,3]{1,0:T(1,128)S(1)} %maximum_multiply_fusion), channel_id=1, replica_groups=mesh['dp'=32,'tensor'=8] {'dp','tensor'}, use_global_device_ids=true, to_apply=%region_24.25 | all-reduce | flops 3 | bytes 24 | tf_op jit(solution)/shard_map/psum | solution.py:57
  (49 shorter events, 28.8 us)
Async XLA Ops:
  7.2 703.6 %reduce-scatter.2.cloned.1.call-start = ((), (), s32[]{:S(2)}) async-start(), calls=%async_computation.1 | async-start | bytes 4718592 | tf_op jit(solution)/shard_map/reduce_scatter | solution.py:20
  7.2 6.0 copy-start.1
  69.8 91.5 %collective-permute-start = (f32[16,128,512]{2,1,0:T(8,128)}, f32[16,128,512]{2,1,0:T(8,128)}, u32[]{:S(2)}, u32[]{:S(2)}) collective-permute-start(f32[16,128,512]{2,1,0:T(8,128)} %select_bitcast_fusion), channel_id=1, source_target_pairs={{0,8},{8,0},{16,24},{24,16},{32,40},{40,32},{48,56},{56,48},{64,72... | collective-permute-start | bytes 12582920 | tf_op jit(solution)/shard_map/ppermute | solution.py:14
  259.8 2.1 copy-start
  259.8 4.0 copy-start.3
  262.4 48.4 %collective-permute-start.1 = (f32[8,128,512]{2,1,0:T(8,128)S(1)}, f32[8,128,512]{2,1,0:T(8,128)}, u32[]{:S(2)}, u32[]{:S(2)}) collective-permute-start(f32[8,128,512]{2,1,0:T(8,128)S(1)} %select_bitcast_fusion.1), channel_id=1, source_target_pairs={{0,16},{8,24},{16,0},{24,8},{32,48},{40,56},{48,32},{56,40},{64,80... | collective-permute-start | bytes 6291464 | tf_op jit(solution)/shard_map/ppermute | solution.py:14
  399.0 24.8 %collective-permute-start.2 = (f32[4,128,512]{2,1,0:T(8,128)S(1)}, f32[4,128,512]{2,1,0:T(8,128)}, u32[]{:S(2)}, u32[]{:S(2)}) collective-permute-start(f32[4,128,512]{2,1,0:T(8,128)S(1)} %select_bitcast_fusion.2), channel_id=1, source_target_pairs={{0,32},{8,40},{16,48},{24,56},{32,0},{40,8},{48,16},{56,24},{64,96... | collective-permute-start | bytes 3145736 | tf_op jit(solution)/shard_map/ppermute | solution.py:14
  507.3 202.7 %copy-start.2 = (f32[128,512]{1,0:T(8,128)S(1)}, f32[128,512]{1,0:T(8,128)}, u32[]{:S(2)}) copy-start(f32[128,512]{1,0:T(8,128)} %param.7) | copy-start | bytes 786436
  507.4 25.1 %collective-permute-start.3 = (f32[2,128,512]{2,1,0:T(8,128)S(1)}, f32[2,128,512]{2,1,0:T(8,128)S(1)}, u32[]{:S(2)}, u32[]{:S(2)}) collective-permute-start(f32[2,128,512]{2,1,0:T(8,128)S(1)} %select_bitcast_fusion.3), channel_id=1, source_target_pairs={{0,64},{8,72},{16,80},{24,88},{32,96},{40,104},{48,112},{56,120},{... | collective-permute-start | bytes 1572872 | tf_op jit(solution)/shard_map/ppermute | solution.py:14
  612.2 17.2 %collective-permute-start.4 = (f32[1,128,512]{2,1,0:T(8,128)S(1)}, f32[1,128,512]{2,1,0:T(8,128)S(1)}, u32[]{:S(2)}, u32[]{:S(2)}) collective-permute-start(f32[1,128,512]{2,1,0:T(8,128)S(1)} %select_bitcast_fusion.4), channel_id=1, source_target_pairs={{0,128},{8,136},{16,144},{24,152},{32,160},{40,168},{48,176},{56,1... | collective-permute-start | bytes 786440 | tf_op jit(solution)/shard_map/ppermute | solution.py:14
Sparse Core Ops, SparseCore 0:
  268.2 35.2 reduce-scatter.1
where the time goes:
time: 721 us; the launch traced here: 720 us
  blocking collectives  376 us (52%)
  waiting for transfers between devices  194 us (27%)
  local copies, waits for them, and re-layouts  52.8 us (7%)
  other arithmetic  45.4 us (6%)
  between operations  27.2 us (4%)
  matrix products  15.9 us (2%)
  starting transfers between devices  8.29 us (1%)
    psum x5, blocking collectives, body(): totals = lax.psum(table, ('dp', 'tensor'))  376 us
    ppermute x5, waiting for transfers between devices, partner(): return lax.ppermute(value, axis, pairs)  194 us
    unnamed x11, local copies, waits for them, and re-layouts  26 us
    reduce_sum x5, other arithmetic, body(): jnp.sum(first * second)  18.2 us
  transfers between devices with their start and end apart: 6, of which 5 were waited for; matrix products, arithmetic and copies ran while one was open for 5% of the time, Pallas kernels for 0%

commit v1 on v0

v1 whole, which is shorter than its diff:
```python
import math

import jax
import jax.numpy as jnp
from jax import lax
from jax.sharding import PartitionSpec as P

ROWS = 512
HI = lax.Precision.HIGHEST


def tree_weights(gram):
    count = gram.shape[0]
    items = jnp.eye(count, dtype=jnp.float32)
    while items.shape[0] > 1:
        first, second = items[0::2], items[1::2]
        first_g = jnp.dot(first, gram, precision=HI)
        second_g = jnp.dot(second, gram, precision=HI)
        cross = jnp.sum(first_g * second, axis=1)
        first_sq = jnp.sum(first_g * first, axis=1)
        second_sq = jnp.sum(second_g * second, axis=1)
        items = (1.0 - cross / (2.0 * first_sq))[:, None] * first + (
            1.0 - cross / (2.0 * second_sq)
        )[:, None] * second
    return items[0], jnp.concatenate([first_sq, second_sq])


def body(inputs, weight, targets, momentum):
    outputs = jnp.dot(inputs, weight, preferred_element_type=jnp.float32)
    error = (outputs - targets.astype(jnp.float32)).astype(jnp.bfloat16)
    summed = lax.psum_scatter(
        lax.dot_general(
            weight, error, (((1,), (1,)), ((), ())), preferred_element_type=jnp.float32
        ).astype(jnp.bfloat16),
        "tensor",
        scatter_dimension=0,
        tiled=True,
    )
    grad = lax.dot_general(
        inputs, error, (((0,), (0,)), ((), ())), preferred_element_type=jnp.float32
    )
    grad = (grad * (1.0 / math.sqrt(ROWS))).astype(jnp.bfloat16)
    groups = lax.axis_size("dp")
    block_rows = grad.shape[0] // groups
    columns = grad.shape[1]
    pieces = lax.all_to_all(
        grad.reshape(groups, block_rows, columns), "dp", split_axis=0, concat_axis=0
    )
    partial = jnp.einsum("gij,hij->gh", pieces, pieces, preferred_element_type=jnp.float32)
    gram = lax.psum(partial, ("dp", "tensor"))
    weights, squares = tree_weights(gram)
    combined = jnp.sum(weights[:, None, None] * pieces.astype(jnp.float32), axis=0)
    tree_norms = jnp.sqrt(squares) / weight.shape[0]
    return (summed, 0.9 * momentum + combined, tree_norms)


def solution(mesh):
    return jax.shard_map(
        body,
        mesh=mesh,
        in_specs=(P("dp", None), P(None, "tensor"), P("dp", "tensor"), P("dp", "tensor")),
        out_specs=(P("tensor", "dp"), P("dp", "tensor"), P()),
        check_vma=False,
    )
```

time: 721 us -> 241 us (0.33)
  blocking collectives: 376 us -> 78.1 us
  waiting for transfers between devices: 194 us -> 86.1 us
  local copies, waits for them, and re-layouts: 52.8 us -> 8.79 us
  other arithmetic: 45.4 us -> 6.16 us
  matrix products: 15.9 us -> 32.6 us
  between operations: 27.2 us -> 16.8 us
    psum x5 -> x1, blocking collectives: 376 us -> 78.1 us  [body(): gram = lax.psum(partial, ('dp', 'tensor'))]
    ppermute x5 -> x0, waiting for transfers between devices: 194 us -> none  [partner(): return lax.ppermute(value, axis, pairs)]
    all_to_all x0 -> x1, waiting for transfers between devices: none -> 86.1 us  [body(): lax.all_to_all(grad.reshape(groups, block_rows, columns), 'dp', split_axi...]
    unnamed x11 -> x5, local copies, waits for them, and re-layouts: 26 us -> 2.05 us
    dot_general x0 -> x11, matrix products: none -> 15.8 us  [the longest x1 12.2 us: body(): jnp.einsum('gij,hij->gh', pieces, pieces, preferred_element_type=jnp.floa...]
    reduce_sum x9 -> x1, other arithmetic: 18.6 us -> 3.17 us  [body(): jnp.sum(weights[:, None, None] * pieces.astype(jnp.float32), axis=0)]
    slice x6 -> x10, local copies, waits for them, and re-layouts: 15 us -> 0.21 us  [tree_weights(): first, second = (items[0::2], items[1::2])]
    all_to_all x0 -> x1, starting transfers between devices: none -> 12.2 us  [body(): lax.all_to_all(grad.reshape(groups, block_rows, columns), 'dp', split_axi...]
  transfers between devices with their start and end apart: 6 -> 2, of which waited for: 5 -> 1; matrix products, arithmetic and copies ran while one was open for 5% -> 12% of each run, Pallas kernels for 0% -> 0%
where the time goes in v1:
time: 241 us
  waiting for transfers between devices  86.1 us (36%)
  blocking collectives  78.1 us (32%)
  matrix products  32.6 us (14%)
  between operations  16.8 us (7%)
  starting transfers between devices  12.4 us (5%)
  local copies, waits for them, and re-layouts  8.79 us (4%)
  other arithmetic  6.16 us (3%)
    all_to_all x1, waiting for transfers between devices, body(): lax.all_to_all(grad.reshape(groups, block_rows, columns), 'dp', split_axi...  86.1 us
    psum x1, blocking collectives, body(): gram = lax.psum(partial, ('dp', 'tensor'))  78.1 us
    dot_general x1, matrix products, body(): jnp.einsum('gij,hij->gh', pieces, pieces, preferred_element_type=jnp.floa...  12.2 us
    all_to_all x1, starting transfers between devices, body(): lax.all_to_all(grad.reshape(groups, block_rows, columns), 'dp', split_axi...  12.2 us
    dot_general x1, matrix products, body(): lax.dot_general(weight, error, (((1,), (1,)), ((), ())), preferred_elemen...  6.54 us
    reshape x1, local copies, waits for them, and re-layouts, body(): grad.reshape(groups, block_rows, columns)  6.52 us
    dot_general x1, matrix products, body(): outputs = jnp.dot(inputs, weight, preferred_element_type=jnp.float32)  5.97 us
  transfers between devices with their start and end apart: 2, of which 1 were waited for; matrix products, arithmetic and copies ran while one was open for 12% of the time, Pallas kernels for 0%

profile of v1, /device:TPU:1, one launch (start us, length us, event | category | flops | bytes accessed | tf_op | source)
XLA Modules:
  0.0 240.9 jit_solution(11511092619309328933)
XLA Ops:
  7.2 6.0 %fusion.4 = bf16[512,512]{1,0:T(8,128)(2,1)S(1)} fusion(bf16[512,4096]{1,0:T(8,128)(2,1)} %param.4, bf16[4096,512]{1,0:T(8,128)(2,1)} %param.5, bf16[512,512]{1,0:T(8,128)(2,1)} %param.6), kind=kOutput, calls=%fused_computation.8 | convolution fusion | flops 2148270080 | bytes 9437184 | tf_op jit(solution)/shard_map/dot_general | solution.py:29
  13.2 4.3 %fusion.1 = bf16[4096,512]{0,1:T(8,128)(2,1)} fusion(bf16[512,512]{1,0:T(8,128)(2,1)S(1)} %fusion.4, bf16[512,4096]{1,0:T(8,128)(2,1)S(1)} %copy-done), kind=kOutput, calls=%fused_computation.4 | convolution fusion | flops 2151677952 | bytes 8912896 | tf_op jit(solution)/shard_map/dot_general | solution.py:39
  17.5 6.5 %copy.13 = bf16[4096,512]{1,0:T(8,128)(2,1)} copy(bf16[4096,512]{0,1:T(8,128)(2,1)} %fusion.1) | data formatting | bytes 8388608 | tf_op jit(solution)/shard_map/reshape | solution.py:47
  24.0 12.2 %all-to-all-start = ((bf16[32,128,512]{2,1,0:T(8,128)(2,1)}), bf16[32,128,512]{2,1,0:T(8,128)(2,1)}, u32[]{:S(2)}, u32[]{:S(2)}) async-start(bf16[32,128,512]{2,1,0:T(8,128)(2,1)} %bitcast.50), calls=%async_computation.1 | async-start | bytes 8388608 | tf_op jit(solution)/shard_map/all_to_all | solution.py:46
  36.2 0.2 reduce-scatter.2.cloned.1.call-start
  36.4 6.5 %fusion = bf16[4096,512]{0,1:T(8,128)(2,1)} fusion(bf16[512,512]{1,0:T(8,128)(2,1)S(1)} %fusion.4, bf16[4096,512]{1,0:T(8,128)(2,1)} %param.5), kind=kOutput, calls=%fused_computation.3 | convolution fusion | flops 2149580800 | bytes 8912896 | tf_op jit(solution)/shard_map/dot_general | solution.py:32
  43.1 86.1 %all-to-all-done = bf16[32,128,512]{2,1,0:T(8,128)(2,1)} async-done(((bf16[32,128,512]{2,1,0:T(8,128)(2,1)}), bf16[32,128,512]{2,1,0:T(8,128)(2,1)}, u32[]{:S(2)}, u32[]{:S(2)}) %all-to-all-start) | async-done | bytes 4194336 | tf_op jit(solution)/shard_map/all_to_all | solution.py:46
  129.2 12.2 %fusion.5 = f32[32,32]{1,0:T(8,128)S(1)} fusion(bf16[32,128,512]{2,1,0:T(8,128)(2,1)} %all-to-all-done), kind=kOutput, calls=%fused_computation.9 | convolution fusion | flops 134217728 | bytes 4198400 | tf_op jit(solution)/shard_map/gij,hij->gh/dot_general | solution.py:49
  141.4 78.1 %psum.7 = f32[32,32]{1,0:T(8,128)S(1)} all-reduce(f32[32,32]{1,0:T(8,128)S(1)} %fusion.5), channel_id=1, replica_groups=mesh['dp'=32,'tensor'=8] {'dp','tensor'}, use_global_device_ids=true, to_apply=%region_1.0 | all-reduce | flops 1024 | bytes 8192 | tf_op jit(solution)/shard_map/psum | solution.py:50
  219.5 0.2 fusion.8
  219.8 0.2 multiply_reduce_fusion.1
  220.0 0.1 multiply_add_fusion.1
  220.1 0.2 fusion.9
  220.4 0.3 multiply_reduce_fusion.3
  220.8 0.2 fusion.10
  221.0 0.3 multiply_reduce_fusion.5
  221.5 0.2 fusion.11
  221.7 0.3 multiply_reduce_fusion.7
  222.1 0.7 multiply_reduce_fusion.9
  223.5 0.7 fusion.12
  226.2 1.9 fusion.14
  228.1 3.2 %multiply_reduce_fusion = f32[128,512]{1,0:T(8,128)S(1)} fusion(bf16[32,128,512]{2,1,0:T(8,128)(2,1)} %all-to-all-done, f32[32]{0:T(128)S(1)} %add_bitcast_fusion), kind=kLoop, calls=%fused_computation | loop fusion | flops 6225920 | bytes 4456576 | tf_op jit(solution)/shard_map/reduce_sum | solution.py:52
  231.3 0.7 multiply_add_fusion
  232.0 2.0 copy.12
  (26 shorter events, 0.5 us)
Async XLA Ops:
  7.2 6.0 %copy-start = (bf16[512,4096]{1,0:T(8,128)(2,1)S(1)}, bf16[512,4096]{1,0:T(8,128)(2,1)}, u32[]{:S(2)}) copy-start(bf16[512,4096]{1,0:T(8,128)(2,1)} %param.4) | copy-start | bytes 12582916
  24.0 105.2 %all-to-all-start = ((bf16[32,128,512]{2,1,0:T(8,128)(2,1)}), bf16[32,128,512]{2,1,0:T(8,128)(2,1)}, u32[]{:S(2)}, u32[]{:S(2)}) async-start(bf16[32,128,512]{2,1,0:T(8,128)(2,1)} %bitcast.50), calls=%async_computation.1 | async-start | bytes 8388608 | tf_op jit(solution)/shard_map/all_to_all | solution.py:46
  36.2 195.9 %reduce-scatter.2.cloned.1.call-start = ((), (), s32[]{:S(2)}) async-start(), calls=%async_computation.2 | async-start | bytes 4718592 | tf_op jit(solution)/shard_map/reduce_scatter | solution.py:31
  43.1 188.2 %copy-start.1 = (f32[128,512]{1,0:T(8,128)S(1)}, f32[128,512]{1,0:T(8,128)}, u32[]{:S(2)}) copy-start(f32[128,512]{1,0:T(8,128)} %param.7) | copy-start | bytes 786436
Sparse Core Ops, SparseCore 0:
  43.1 40.1 reduce-scatter.1

commit v2 on v1

v2 whole, which is shorter than its diff:
```python
import functools
import math

import jax
import jax.numpy as jnp
from jax import lax
from jax.experimental import pallas as pl
from jax.experimental.pallas import tpu as pltpu
from jax.sharding import PartitionSpec as P

MESH = pl.DeviceIdType.MESH
NZ, NY, NX, NC = 8, 4, 4, 2
NT = NX * NC
F32, BF16 = jnp.float32, jnp.bfloat16
KCHUNKS = 4
YPAIRS = [(i, j) for i in range(NY) for j in range(i, NY)]
ZPAIRS = [(i, j) for i in range(NZ) for j in range(i, NZ)]


def tree(gram, pairs):
    count = max(j for _, j in pairs) + 1
    value = {}
    for at, (i, j) in enumerate(pairs):
        value[i, j] = value[j, i] = gram[at]
    items = [{i: None} for i in range(count)]

    def weighted(term, coefficient):
        return term if coefficient is None else term * coefficient

    def inner(first, second):
        total = None
        for i, a in first.items():
            for j, c in second.items():
                term = weighted(weighted(value[i, j], a), c)
                total = term if total is None else total + term
        return total

    while len(items) > 1:
        merged = []
        for at in range(0, len(items), 2):
            first, second = items[at], items[at + 1]
            cross, first_sq, second_sq = inner(first, second), inner(first, first), inner(second, second)
            left = 1.0 - cross / (2.0 * first_sq)
            right = 1.0 - cross / (2.0 * second_sq)
            item = {i: weighted(left, a) for i, a in first.items()}
            item.update({i: weighted(right, c) for i, c in second.items()})
            merged.append(item)
        items = merged
    return [items[0][i] for i in range(count)], first_sq, second_sq


def kernel(
    inputs, weight, targets,
    ig_out, comb_out, norm_out,
    xin, w, tg, acc, gin, et, psend, precv, ppart, xrecv, gbuf, zsend, zrecv,
    gsum, yred, tred, zred, mine,
    ld_sem, own_sem, iy_send, iy_recv, ix_send, ix_recv, is_send, is_recv,
    e_send, e_recv, p_send, p_recv, q_send, q_recv, z_send, z_recv, r_send, r_recv,
):
    dp, t = lax.axis_index("dp"), lax.axis_index("tensor")
    z, y, x, c = dp // NY, dp % NY, t // NC, t % NC
    rows, width = inputs.shape
    cols = weight.shape[1]
    kc = width // KCHUNKS
    part_rows = rows // NT
    block = width // (NZ * NY)
    wide = block * NZ

    def at(dz=0, dy=0, dt=None):
        return ((z + dz) % NZ * NY + (y + dy) % NY, t if dt is None else (t + dt) % NT)

    def at_x(dx, core):
        return (dp, (x + dx) % NX * NC + core)

    loads = []
    for i in range(KCHUNKS):
        a = pltpu.make_async_copy(inputs.at[:, i * kc:(i + 1) * kc], xin.at[:, i * kc:(i + 1) * kc], ld_sem.at[2 * i])
        b = pltpu.make_async_copy(weight.at[i * kc:(i + 1) * kc], w.at[i * kc:(i + 1) * kc], ld_sem.at[2 * i + 1])
        a.start()
        b.start()
        loads.append((a, b))
    tg_load = pltpu.make_async_copy(targets, tg, ld_sem.at[2 * KCHUNKS])
    tg_load.start()

    barrier = pltpu.get_barrier_semaphore()
    peers = [at(dz=k) for k in range(1, NZ)] + [at(dy=k) for k in range(1, NY)] + [at(dt=k) for k in range(1, NT)]
    for peer in peers:
        pl.semaphore_signal(barrier, inc=1, device_id=peer, device_id_type=MESH)
    pl.semaphore_wait(barrier, len(peers))

    def remote(src, dst, send, recv, peer):
        return pltpu.make_async_remote_copy(
            src_ref=src, dst_ref=dst, send_sem=send, recv_sem=recv, device_id=peer, device_id_type=MESH
        )

    my_rows = pl.ds(pl.multiple_of(t * part_rows, part_rows), part_rows)
    for k in (2, 1, 3):
        for b in range(NZ):
            col = pl.multiple_of((b * NY + (y + k) % NY) * block, block)
            remote(
                inputs.at[my_rows, pl.ds(col, block)], gin.at[y, my_rows, b * block:(b + 1) * block],
                iy_send.at[k - 1], iy_recv.at[3 - k], at(dy=k),
            ).start()
    for b in range(NZ):
        col = pl.multiple_of((b * NY + y) * block, block)
        pltpu.make_async_copy(inputs.at[:, pl.ds(col, block)], gin.at[y, :, b * block:(b + 1) * block], own_sem).start()

    for i, (a, b) in enumerate(loads):
        a.wait()
        b.wait()
        part = jnp.dot(xin[:, i * kc:(i + 1) * kc], w[i * kc:(i + 1) * kc, :], preferred_element_type=F32)
        if i == 0:
            acc[...] = part
        else:
            acc[...] += part
    tg_load.wait()
    et[y] = jnp.transpose((acc[...] - tg[...].astype(F32)).astype(BF16))

    half = cols // 2
    low, high = pl.ds(0, half), pl.ds(half, half)
    right, left, across = (y + 1) % NY, (y + 3) % NY, (y + 2) % NY

    def send_error(index, sem, part, dy):
        copy = remote(et.at[index, part], et.at[index, part], e_send.at[sem], e_recv.at[sem], at(dy=dy))
        copy.start()
        return copy

    e_copies = [
        send_error(y, 0, low, 3),
        send_error(y, 3, high, 1),
        send_error(y, 1, high, 3),
        send_error(y, 2, low, 1),
    ]

    def e_wait(index, sem, part):
        remote(et.at[index, part], et.at[index, part], e_send.at[sem], e_recv.at[sem], at(dy=1)).wait_recv()

    sib = at_x(0, 1 - c)
    for k in (1, 2, 3):
        remote(
            gin.at[(y + k) % NY, my_rows], gin.at[(y + k) % NY, my_rows], iy_send.at[k - 1], iy_recv.at[k - 1], at(dy=k)
        ).wait_recv()
    ix_copies, is_copies = [], []

    def share(rows_at, sends, recvs, base, peer, out):
        for k in (1, 2, 3):
            ref = gin.at[(y + k) % NY, rows_at]
            copy = remote(ref, ref, sends.at[base + k - 1], recvs.at[base + k - 1], peer)
            copy.start()
            out.append(copy)

    for j in (2, 1, 3):
        share(my_rows, ix_send, ix_recv, (3 - j) * 3, at_x(j, c), ix_copies)
    share(my_rows, is_send, is_recv, 0, sib, is_copies)

    p_copies = []
    for j in range(NX):
        start = pl.multiple_of(((x + j) % NX * NC + 1 - c) * cols, cols)
        psend[j] = jnp.dot(w[pl.ds(start, cols), :], et[y], preferred_element_type=F32).astype(BF16)
        copy = remote(psend.at[j], precv.at[j], p_send.at[j], p_recv.at[j], sib)
        copy.start()
        p_copies.append(copy)
    for j in range(NX):
        start = pl.multiple_of(((x + j) % NX * NC + c) * cols, cols)
        ppart[j] = jnp.dot(w[pl.ds(start, cols), :], et[y], preferred_element_type=F32).astype(BF16)

    def gradient(index):
        gbuf[index] = jnp.dot(et[index], gin[index], preferred_element_type=F32)

    pltpu.make_async_copy(gin.at[y], gin.at[y], own_sem).wait()
    gradient(y)

    e_wait(right, 0, low)
    e_copies.append(send_error(right, 4, low, 3))
    e_wait(left, 3, high)
    e_copies.append(send_error(left, 5, high, 1))

    for j in range(NX):
        p_copies[j].wait_recv()
        ppart[j] = (ppart[j].astype(F32) + precv[j].astype(F32)).astype(BF16)

    for j in (1, 3, 2):
        rows_at = pl.ds(pl.multiple_of(((x + j) % NX * NC + c) * part_rows, part_rows), part_rows)
        for k in (1, 2, 3):
            ref = gin.at[(y + k) % NY, rows_at]
            remote(ref, ref, ix_send.at[0], ix_recv.at[(j - 1) * 3 + k - 1], sib).wait_recv()
        share(rows_at, is_send, is_recv, j * 3, sib, is_copies)

    q_copies = []
    for j in (2, 1, 3):
        copy = remote(ppart.at[j], xrecv.at[3 - j], q_send.at[j - 1], q_recv.at[3 - j], at_x(j, c))
        copy.start()
        q_copies.append(copy)

    for copy in is_copies:
        copy.wait_recv()
    e_wait(right, 1, high)
    gradient(right)
    e_wait(left, 2, low)
    gradient(left)
    e_wait(across, 4, low)
    e_wait(across, 5, high)
    gradient(across)

    gsum[...] = jnp.zeros_like(gsum)
    ones = jnp.ones((8, 128), F32)
    lane = lax.broadcasted_iota(jnp.int32, (8, 128), 1)

    def to_lanes(sums):
        for p, value in enumerate(sums):
            gsum[p:p + 1, :] = jnp.sum(value, axis=0, keepdims=True)
        return lax.dot_general(
            ones, gsum[...], (((1,), (1,)), ((), ())), precision=lax.Precision.HIGHEST, preferred_element_type=F32
        )

    def reduce_stage(value, slot, buffer, count, me, peer_of):
        mine[slot] = value
        buffer[me] = value
        for k in range(1, count):
            remote(mine.at[slot], buffer.at[me], r_send.at[slot], r_recv.at[slot], peer_of(k)).start()
        some = buffer.at[0:count - 1]
        remote(some, some, r_send.at[slot], r_recv.at[slot], peer_of(1)).wait()
        total = buffer[0]
        for k in range(1, count):
            total = total + buffer[k]
        return total

    def pick(vec, count):
        return [
            jnp.sum(jnp.where(lane == p, vec, 0.0), axis=1, keepdims=True)[0:1, :] for p in range(count)
        ]

    def fold(value):
        total = value[:, 0:128]
        for l in range(1, value.shape[1] // 128):
            total = total + value[:, l * 128:(l + 1) * 128]
        return total

    def y_step(i, sums):
        at_rows = pl.ds(pl.multiple_of(i * 8, 8), 8)
        items = [gbuf[k, at_rows, :] for k in range(NY)]
        return tuple(s + fold(items[a] * items[b]) for s, (a, b) in zip(sums, YPAIRS))

    zero = jnp.zeros((8, 128), F32)
    vec = to_lanes(lax.fori_loop(0, cols // 8, y_step, (zero,) * len(YPAIRS)))
    vec = reduce_stage(vec, 0, yred.at[0], NY, y, lambda k: at(dy=k))
    vec = reduce_stage(vec, 1, tred.at[0], NT, t, lambda k: at(dt=k))
    weights, _, _ = tree(pick(vec, len(YPAIRS)), YPAIRS)
    weights = [v * (1.0 / math.sqrt(rows)) for v in weights]

    def combine(b):
        lanes = pl.ds(pl.multiple_of(b * block, block), block)
        total = weights[0] * gbuf[0, :, lanes]
        for k in range(1, NY):
            total = total + weights[k] * gbuf[k, :, lanes]
        return total.astype(BF16)

    z_copies = []
    for k in (4, 3, 5, 2, 6, 1, 7):
        b = (z + k) % NZ
        zsend[k - 1] = combine(b)
        copy = remote(zsend.at[k - 1], zrecv.at[z], z_send.at[k - 1], z_recv.at[NZ - 1 - k], at(dz=k))
        copy.start()
        z_copies.append(copy)
    zrecv[z] = combine(z)

    for copy in q_copies:
        copy.wait_recv()
    total = ppart[0].astype(F32)
    for j in range(NX - 1):
        total = total + xrecv[j].astype(F32)
    ig_out[...] = total.astype(BF16)

    for k in range(1, NZ):
        remote(zrecv.at[(z + k) % NZ], zrecv.at[(z + k) % NZ], z_send.at[k - 1], z_recv.at[k - 1], at(dz=1)).wait_recv()

    def z_step(i, sums):
        at_rows = pl.ds(pl.multiple_of(i * 16, 16), 16)
        items = [zrecv[k, at_rows, :].astype(F32) for k in range(NZ)]
        out = []
        for s, (a, b) in zip(sums, ZPAIRS):
            product = items[a] * items[b]
            out.append(s + product[0:8] + product[8:16])
        return tuple(out)

    vec = to_lanes(lax.fori_loop(0, cols // 16, z_step, (zero,) * len(ZPAIRS)))
    vec = reduce_stage(vec, 2, zred, NZ, z, lambda k: at(dz=k))
    vec = reduce_stage(vec, 3, yred.at[1], NY, y, lambda k: at(dy=k))
    vec = reduce_stage(vec, 4, tred.at[1], NT, t, lambda k: at(dt=k))
    weights, first_sq, second_sq = tree(pick(vec, len(ZPAIRS)), ZPAIRS)
    total = weights[0] * zrecv[0].astype(F32)
    for k in range(1, NZ):
        total = total + weights[k] * zrecv[k].astype(F32)
    comb_out[...] = jnp.transpose(total)
    norm_out[...] = jnp.where(lane == 0, jnp.sqrt(first_sq), jnp.sqrt(second_sq)) * (1.0 / width)

    for k in (1, 2, 3):
        ref = gin.at[(y + k) % NY, my_rows]
        remote(ref, ref, iy_send.at[k - 1], iy_recv.at[k - 1], at(dy=k)).wait_send()
    for copy in e_copies + ix_copies + is_copies + p_copies + q_copies + z_copies:
        copy.wait_send()


def body(inputs, weight, targets, momentum):
    rows, width = inputs.shape
    cols = weight.shape[1]
    block = width // (NZ * NY)
    wide = block * NZ
    dma = pltpu.SemaphoreType.DMA
    any_spec = pl.BlockSpec(memory_space=pl.ANY)
    vmem = pl.BlockSpec(memory_space=pltpu.VMEM)
    summed, combined, norms = pl.pallas_call(
        kernel,
        out_shape=(
            jax.ShapeDtypeStruct((cols, rows), BF16),
            jax.ShapeDtypeStruct((block, cols), F32),
            jax.ShapeDtypeStruct((8, 128), F32),
        ),
        in_specs=[any_spec] * 3,
        out_specs=(vmem, vmem, vmem),
        scratch_shapes=[
            pltpu.VMEM((rows, width), BF16),
            pltpu.VMEM((width, cols), BF16),
            pltpu.VMEM((rows, cols), BF16),
            pltpu.VMEM((rows, cols), F32),
            pltpu.VMEM((NY, rows, wide), BF16),
            pltpu.VMEM((NY, cols, rows), BF16),
            pltpu.VMEM((NX, cols, rows), BF16),
            pltpu.VMEM((NX, cols, rows), BF16),
            pltpu.VMEM((NX, cols, rows), BF16),
            pltpu.VMEM((NX - 1, cols, rows), BF16),
            pltpu.VMEM((NY, cols, wide), F32),
            pltpu.VMEM((NZ - 1, cols, block), BF16),
            pltpu.VMEM((NZ, cols, block), BF16),
            pltpu.VMEM((128, 128), F32),
            pltpu.VMEM((2, NY, 8, 128), F32),
            pltpu.VMEM((2, NT, 8, 128), F32),
            pltpu.VMEM((NZ, 8, 128), F32),
            pltpu.VMEM((5, 8, 128), F32),
            dma((2 * KCHUNKS + 1,)),
            dma,
            dma((3,)), dma((3,)),
            dma((9,)), dma((9,)),
            dma((12,)), dma((12,)),
            dma((6,)), dma((6,)),
            dma((NX,)), dma((NX,)),
            dma((3,)), dma((3,)),
            dma((NZ - 1,)), dma((NZ - 1,)),
            dma((5,)), dma((5,)),
        ],
        compiler_params=pltpu.CompilerParams(
            collective_id=0, has_side_effects=True, vmem_limit_bytes=60 * 2**20
        ),
    )(inputs, weight, targets)
    return (summed, 0.9 * momentum + combined, norms[0, :2])


def solution(mesh):
    return jax.shard_map(
        body,
        mesh=mesh,
        in_specs=(P("dp", None), P(None, "tensor"), P("dp", "tensor"), P("dp", "tensor")),
        out_specs=(P("tensor", "dp"), P("dp", "tensor"), P()),
        check_vma=False,
    )
```

time: 241 us -> 108 us (0.45)
  Pallas kernels: 0 us -> 103 us
  waiting for transfers between devices: 86.1 us -> 0 us
  blocking collectives: 78.1 us -> 0 us
  matrix products: 32.6 us -> 0 us
  between operations: 16.8 us -> 0.65 us
  starting transfers between devices: 12.4 us -> 0 us
  local copies, waits for them, and re-layouts: 8.79 us -> 3.06 us
  other arithmetic: 6.16 us -> 1.69 us
    pallas_call x0 -> x1, Pallas kernels: none -> 103 us  [body(): pl.pallas_call(kernel, out_shape=(jax.ShapeDtypeStruct((cols, rows), BF16...]
    all_to_all x1 -> x0, waiting for transfers between devices: 86.1 us -> none  [body(): lax.all_to_all(grad.reshape(groups, block_rows, columns), 'dp', split_axi...]
    psum x1 -> x0, blocking collectives: 78.1 us -> none  [body(): gram = lax.psum(partial, ('dp', 'tensor'))]
    dot_general x14 -> x0, matrix products: 32.6 us -> none  [the longest x1 12.2 us: body(): jnp.einsum('gij,hij->gh', pieces, pieces, preferred_element_type=jnp.floa...]
    all_to_all x1 -> x0, starting transfers between devices: 12.2 us -> none  [body(): lax.all_to_all(grad.reshape(groups, block_rows, columns), 'dp', split_axi...]
    reshape x1 -> x0, local copies, waits for them, and re-layouts: 6.52 us -> none  [body(): grad.reshape(groups, block_rows, columns)]
    reduce_sum x1 -> x0, other arithmetic: 3.17 us -> none  [body(): jnp.sum(weights[:, None, None] * pieces.astype(jnp.float32), axis=0)]
  transfers between devices with their start and end apart: 2 -> 0, of which waited for: 1 -> 0; matrix products, arithmetic and copies ran while one was open for 12% -> 0% of each run, Pallas kernels for 0% -> 0%
where the time goes in v2:
time: 108 us
  Pallas kernels  103 us (95%)
  local copies, waits for them, and re-layouts  3.06 us (3%)
  other arithmetic  1.69 us (2%)
    pallas_call x1, Pallas kernels, body(): pl.pallas_call(kernel, out_shape=(jax.ShapeDtypeStruct((cols, rows), BF16...  103 us

profile of v2, /device:TPU:1, one launch (start us, length us, event | category | flops | bytes accessed | tf_op | source)
XLA Modules:
  0.0 108.1 jit_solution(15637776303357316147)
XLA Ops:
  0.6 0.0 copy-start
  0.6 102.7 %shard_map.67 = (bf16[512,512]{1,0:T(8,128)(2,1)}, f32[128,512]{1,0:T(8,128)}, f32[8,128]{1,0:T(8,128)}) custom-call(bf16[512,4096]{1,0:T(8,128)(2,1)} %inputs.1, bf16[4096,512]{1,0:T(8,128)(2,1)} %weight.1, bf16[512,512]{1,0:T(8,128)(2,1)} %targets.1), custom_call_target="tpu_custom_call" | custom-call | tf_op jit(solution)/shard_map/pallas_call | solution.py:312
  103.4 1.2 %slice_bitcast_fusion = f32[2]{0:T(128)} fusion(f32[8,128]{1,0:T(8,128)} %get-tuple-element.8), kind=kLoop, calls=%fused_computation.1 | loop fusion | bytes 16 | tf_op jit(solution)/shard_map/squeeze | solution.py:355
  104.6 0.0 copy-done
  104.6 1.7 %multiply_add_fusion = f32[128,512]{1,0:T(8,128)} fusion(f32[128,512]{1,0:T(8,128)} %get-tuple-element.7, f32[128,512]{1,0:T(8,128)S(1)} %copy-done), kind=kLoop, calls=%fused_computation | loop fusion | flops 131072 | bytes 786432 | tf_op jit(solution)/shard_map/add | solution.py:355
  106.3 1.9 %copy.8 = bf16[512,512]{1,0:T(8,128)(2,1)} copy(bf16[512,512]{1,0:T(8,128)(2,1)} %get-tuple-element.12) | data formatting | bytes 1048576
Async XLA Ops:
  0.6 103.9 %copy-start = (f32[128,512]{1,0:T(8,128)S(1)}, f32[128,512]{1,0:T(8,128)}, u32[]{:S(2)}) copy-start(f32[128,512]{1,0:T(8,128)} %param.7) | copy-start | bytes 786436

commit v3 on v2

--- a/solution.py
+++ b/solution.py
@@ -52,9 +52,10 @@
 def kernel(
     inputs, weight, targets,
     ig_out, comb_out, norm_out,
+    ig, comb, norm, gacc,
     xin, w, tg, acc, gin, et, psend, precv, ppart, xrecv, gbuf, zsend, zrecv,
     gsum, yred, tred, zred, mine,
-    ld_sem, own_sem, iy_send, iy_recv, ix_send, ix_recv, is_send, is_recv,
+    ld_sem, out_sem, own_sem, iy_send, iy_recv, ix_send, ix_recv, is_send, is_recv,
     e_send, e_recv, p_send, p_recv, q_send, q_recv, z_send, z_recv, r_send, r_recv,
 ):
     dp, t = lax.axis_index("dp"), lax.axis_index("tensor")
@@ -94,7 +95,7 @@
         )
 
     my_rows = pl.ds(pl.multiple_of(t * part_rows, part_rows), part_rows)
-    for k in (2, 1, 3):
+    for k in (1, 3, 2):
         for b in range(NZ):
             col = pl.multiple_of((b * NY + (y + k) % NY) * block, block)
             remote(
@@ -136,22 +137,36 @@
         remote(et.at[index, part], et.at[index, part], e_send.at[sem], e_recv.at[sem], at(dy=1)).wait_recv()
 
     sib = at_x(0, 1 - c)
-    for k in (1, 2, 3):
-        remote(
-            gin.at[(y + k) % NY, my_rows], gin.at[(y + k) % NY, my_rows], iy_send.at[k - 1], iy_recv.at[k - 1], at(dy=k)
-        ).wait_recv()
-    ix_copies, is_copies = [], []
-
-    def share(rows_at, sends, recvs, base, peer, out):
-        for k in (1, 2, 3):
-            ref = gin.at[(y + k) % NY, rows_at]
-            copy = remote(ref, ref, sends.at[base + k - 1], recvs.at[base + k - 1], peer)
-            copy.start()
-            out.append(copy)
-
-    for j in (2, 1, 3):
-        share(my_rows, ix_send, ix_recv, (3 - j) * 3, at_x(j, c), ix_copies)
-    share(my_rows, is_send, is_recv, 0, sib, is_copies)
+    def rows_of(dx, core):
+        return pl.multiple_of(((x + dx) % NX * NC + core) * part_rows, part_rows)
+
+    sub = part_rows // 2
+    copies = []
+
+    def share(k, start, count, sends, recvs, sem, peer):
+        ref = gin.at[(y + k) % NY, pl.ds(start, count)]
+        copy = remote(ref, ref, sends.at[sem], recvs.at[sem], peer)
+        copy.start()
+        copies.append(copy)
+
+    def shared(k, start, count, sends, recvs, sem):
+        ref = gin.at[(y + k) % NY, pl.ds(start, count)]
+        remote(ref, ref, sends.at[sem], recvs.at[sem], sib).wait_recv()
+
+    mine_low = rows_of(0, c)
+    mine_high = mine_low + sub
+    right_low = rows_of(1, c)
+    left_low = rows_of(3, c)
+    across_low = rows_of(2, c)
+    order = (1, 3, 2)
+    for k in order:
+        ref = gin.at[(y + k) % NY, my_rows]
+        remote(ref, ref, iy_send.at[k - 1], iy_recv.at[k - 1], at(dy=k)).wait_recv()
+        share(k, mine_low, sub, ix_send, ix_recv, k - 1, at_x(3, c))
+        share(k, mine_high, sub, ix_send, ix_recv, 6 + k - 1, at_x(1, c))
+        share(k, mine_high, sub, ix_send, ix_recv, 3 + k - 1, at_x(3, c))
+        share(k, mine_low, sub, ix_send, ix_recv, 9 + k - 1, at_x(1, c))
+        share(k, mine_low, part_rows, is_send, is_recv, k - 1, sib)
 
     p_copies = []
     for j in range(NX):
@@ -170,37 +185,63 @@
     pltpu.make_async_copy(gin.at[y], gin.at[y], own_sem).wait()
     gradient(y)
 
+    for k in order:
+        shared(k, right_low, sub, ix_send, ix_recv, k - 1)
+        share(k, right_low, sub, ix_send, ix_recv, 12 + k - 1, at_x(3, c))
+        shared(k, left_low + sub, sub, ix_send, ix_recv, 6 + k - 1)
+        share(k, left_low + sub, sub, ix_send, ix_recv, 15 + k - 1, at_x(1, c))
     e_wait(right, 0, low)
     e_copies.append(send_error(right, 4, low, 3))
     e_wait(left, 3, high)
     e_copies.append(send_error(left, 5, high, 1))
-
     for j in range(NX):
         p_copies[j].wait_recv()
         ppart[j] = (ppart[j].astype(F32) + precv[j].astype(F32)).astype(BF16)
-
-    for j in (1, 3, 2):
-        rows_at = pl.ds(pl.multiple_of(((x + j) % NX * NC + c) * part_rows, part_rows), part_rows)
-        for k in (1, 2, 3):
-            ref = gin.at[(y + k) % NY, rows_at]
-            remote(ref, ref, ix_send.at[0], ix_recv.at[(j - 1) * 3 + k - 1], sib).wait_recv()
-        share(rows_at, is_send, is_recv, j * 3, sib, is_copies)
-
-    q_copies = []
-    for j in (2, 1, 3):
-        copy = remote(ppart.at[j], xrecv.at[3 - j], q_send.at[j - 1], q_recv.at[3 - j], at_x(j, c))
-        copy.start()
-        q_copies.append(copy)
-
-    for copy in is_copies:
-        copy.wait_recv()
+    for k in order:
+        shared(k, right_low + sub, sub, ix_send, ix_recv, 3 + k - 1)
+        share(k, right_low, part_rows, is_send, is_recv, 3 + k - 1, sib)
+        shared(k, left_low, sub, ix_send, ix_recv, 9 + k - 1)
+        share(k, left_low, part_rows, is_send, is_recv, 6 + k - 1, sib)
+    for k in order:
+        shared(k, across_low, sub, ix_send, ix_recv, 12 + k - 1)
+        shared(k, across_low + sub, sub, ix_send, ix_recv, 15 + k - 1)
+        share(k, across_low, part_rows, is_send, is_recv, 9 + k - 1, sib)
+
+    def inputs_wait(k):
+        for n, dx in enumerate((0, 1, 3, 2)):
+            shared(k, rows_of(dx, 1 - c), part_rows, is_send, is_recv, 3 * n + k - 1)
+
+    def fold(value):
+        total = value[:, 0:128]
+        for l in range(1, value.shape[1] // 128):
+            total = total + value[:, l * 128:(l + 1) * 128]
+        return total
+
+    zero = jnp.zeros((8, 128), F32)
+
+    def inner_products(items, pairs):
+        def step(i, sums):
+            at_rows = pl.ds(pl.multiple_of(i * 8, 8), 8)
+            values = [gbuf[k, at_rows, :] for k in items]
+            return tuple(s + fold(values[a] * values[b]) for s, (a, b) in zip(sums, pairs))
+
+        sums = lax.fori_loop(0, cols // 8, step, (zero,) * len(pairs))
+        for value, (a, b) in zip(sums, pairs):
+            low_index, high_index = jnp.minimum(items[a], items[b]), jnp.maximum(items[a], items[b])
+            gacc[low_index * NY + high_index] = value
+
     e_wait(right, 1, high)
+    inputs_wait(1)
     gradient(right)
     e_wait(left, 2, low)
+    inputs_wait(3)
     gradient(left)
+    inner_products([y, right, left], [(0, 0), (0, 1), (0, 2), (1, 1), (1, 2), (2, 2)])
+    inputs_wait(2)
     e_wait(across, 4, low)
     e_wait(across, 5, high)
     gradient(across)
+    inner_products([across, y, right, left], [(0, 0), (0, 1), (0, 2), (0, 3)])
 
     gsum[...] = jnp.zeros_like(gsum)
     ones = jnp.ones((8, 128), F32)
@@ -230,19 +271,7 @@
             jnp.sum(jnp.where(lane == p, vec, 0.0), axis=1, keepdims=True)[0:1, :] for p in range(count)
         ]
 
-    def fold(value):
-        total = value[:, 0:128]
-        for l in range(1, value.shape[1] // 128):
-            total = total + value[:, l * 128:(l + 1) * 128]
-        return total
-
-    def y_step(i, sums):
-        at_rows = pl.ds(pl.multiple_of(i * 8, 8), 8)
-        items = [gbuf[k, at_rows, :] for k in range(NY)]
-        return tuple(s + fold(items[a] * items[b]) for s, (a, b) in zip(sums, YPAIRS))
-
-    zero = jnp.zeros((8, 128), F32)
-    vec = to_lanes(lax.fori_loop(0, cols // 8, y_step, (zero,) * len(YPAIRS)))
+    vec = to_lanes([gacc[a * NY + b] for a, b in YPAIRS])
     vec = reduce_stage(vec, 0, yred.at[0], NY, y, lambda k: at(dy=k))
     vec = reduce_stage(vec, 1, tred.at[0], NT, t, lambda k: at(dt=k))
     weights, _, _ = tree(pick(vec, len(YPAIRS)), YPAIRS)
@@ -264,12 +293,26 @@
         z_copies.append(copy)
     zrecv[z] = combine(z)
 
+    q_copies = []
+    for j in (2, 1, 3):
+        copy = remote(ppart.at[j], xrecv.at[3 - j], q_send.at[j - 1], q_recv.at[3 - j], at_x(j, c))
+        copy.start()
+        q_copies.append(copy)
+    for k in (1, 2, 3):
+        ref = gin.at[(y + k) % NY, my_rows]
+        remote(ref, ref, iy_send.at[k - 1], iy_recv.at[k - 1], at(dy=k)).wait_send()
+    for copy in e_copies + copies + p_copies:
+        copy.wait_send()
     for copy in q_copies:
         copy.wait_recv()
     total = ppart[0].astype(F32)
     for j in range(NX - 1):
         total = total + xrecv[j].astype(F32)
-    ig_out[...] = total.astype(BF16)
+    ig[...] = total.astype(BF16)
+    ig_copy = pltpu.make_async_copy(ig, ig_out, out_sem.at[0])
+    ig_copy.start()
+    for copy in q_copies:
+        copy.wait_send()
 
     for k in range(1, NZ):
         remote(zrecv.at[(z + k) % NZ], zrecv.at[(z + k) % NZ], z_send.at[k - 1], z_recv.at[k - 1], at(dz=1)).wait_recv()
@@ -291,14 +334,24 @@
     total = weights[0] * zrecv[0].astype(F32)
     for k in range(1, NZ):
         total = total + weights[k] * zrecv[k].astype(F32)
-    comb_out[...] = jnp.transpose(total)
-    norm_out[...] = jnp.where(lane == 0, jnp.sqrt(first_sq), jnp.sqrt(second_sq)) * (1.0 / width)
-
-    for k in (1, 2, 3):
-        ref = gin.at[(y + k) % NY, my_rows]
-        remote(ref, ref, iy_send.at[k - 1], iy_recv.at[k - 1], at(dy=k)).wait_send()
-    for copy in e_copies + ix_copies + is_copies + p_copies + q_copies + z_copies:
+    comb[...] = jnp.transpose(total)
+    comb_copy = pltpu.make_async_copy(comb, comb_out, out_sem.at[1])
+    comb_copy.start()
+    norm[...] = jnp.where(lane == 0, jnp.sqrt(first_sq), jnp.sqrt(second_sq)) * (1.0 / width)
+    norm_copy = pltpu.make_async_copy(norm, norm_out, out_sem.at[2])
+    norm_copy.start()
+    for copy in z_copies:
         copy.wait_send()
+    ig_copy.wait()
+    comb_copy.wait()
+    norm_copy.wait()
+
+
+def finish(ig, comb, norm, momentum, ig_out, momentum_out, norm_out):
+    ig_out[...] = ig[...]
+    momentum_out[...] = 0.9 * momentum[...] + comb[...]
+    norm_out[0] = norm[0, 0]
+    norm_out[1] = norm[0, 1]
 
 
 def body(inputs, weight, targets, momentum):
@@ -317,8 +370,12 @@
             jax.ShapeDtypeStruct((8, 128), F32),
         ),
         in_specs=[any_spec] * 3,
-        out_specs=(vmem, vmem, vmem),
+        out_specs=(any_spec,) * 3,
         scratch_shapes=[
+            pltpu.VMEM((cols, rows), BF16),
+            pltpu.VMEM((block, cols), F32),
+            pltpu.VMEM((8, 128), F32),
+            pltpu.VMEM((NY * NY, 8, 128), F32),
             pltpu.VMEM((rows, width), BF16),
             pltpu.VMEM((width, cols), BF16),
             pltpu.VMEM((rows, cols), BF16),
@@ -338,9 +395,10 @@
             pltpu.VMEM((NZ, 8, 128), F32),
             pltpu.VMEM((5, 8, 128), F32),
             dma((2 * KCHUNKS + 1,)),
+            dma((3,)),
             dma,
             dma((3,)), dma((3,)),
-            dma((9,)), dma((9,)),
+            dma((18,)), dma((18,)),
             dma((12,)), dma((12,)),
             dma((6,)), dma((6,)),
             dma((NX,)), dma((NX,)),
@@ -352,7 +410,17 @@
             collective_id=0, has_side_effects=True, vmem_limit_bytes=60 * 2**20
         ),
     )(inputs, weight, targets)
-    return (summed, 0.9 * momentum + combined, norms[0, :2])
+    smem = pl.BlockSpec(memory_space=pltpu.SMEM)
+    return pl.pallas_call(
+        finish,
+        out_shape=(
+            jax.ShapeDtypeStruct((cols, rows), BF16),
+            jax.ShapeDtypeStruct((block, cols), F32),
+            jax.ShapeDtypeStruct((2,), F32),
+        ),
+        in_specs=[vmem, vmem, smem, vmem],
+        out_specs=(vmem, vmem, smem),
+    )(summed, combined, norms, momentum)
 
 
 def solution(mesh):

time: 108 us -> 88.6 us (0.82)
  Pallas kernels: 103 us -> 87.8 us
  local copies, waits for them, and re-layouts: 3.06 us -> 0 us
  other arithmetic: 1.69 us -> 0 us
    pallas_call x1, Pallas kernels: 103 us -> 85.7 us  [body(): pl.pallas_call(kernel, out_shape=(jax.ShapeDtypeStruct((cols, rows), BF16...]
    pallas_call x0 -> x1, Pallas kernels: none -> 2.12 us  [body(): pl.pallas_call(finish, out_shape=(jax.ShapeDtypeStruct((cols, rows), BF16...]
    unnamed x3 -> x0, local copies, waits for them, and re-layouts: 1.87 us -> none
    add x1 -> x0, other arithmetic: 1.69 us -> none  [body(): return (summed, 0.9 * momentum + combined, norms[0, :2])]
    squeeze x1 -> x0, local copies, waits for them, and re-layouts: 1.18 us -> none  [body(): return (summed, 0.9 * momentum + combined, norms[0, :2])]
where the time goes in v3:
time: 88.6 us; the launch traced here: 88.5 us
  Pallas kernels  87.8 us (99%)
    pallas_call x1, Pallas kernels, body(): pl.pallas_call(kernel, out_shape=(jax.ShapeDtypeStruct((cols, rows), BF16...  85.7 us
    pallas_call x1, Pallas kernels, body(): pl.pallas_call(finish, out_shape=(jax.ShapeDtypeStruct((cols, rows), BF16...  2.12 us

profile of v3, /device:TPU:1, one launch (start us, length us, event | category | flops | bytes accessed | tf_op | source)
XLA Modules:
  0.0 88.5 jit_solution(2326262486096192376)
XLA Ops:
  0.6 85.7 %shard_map.67 = (bf16[512,512]{1,0:T(8,128)(2,1)}, f32[128,512]{1,0:T(8,128)}, f32[8,128]{1,0:T(8,128)}) custom-call(bf16[512,4096]{1,0:T(8,128)(2,1)} %inputs.1, bf16[4096,512]{1,0:T(8,128)(2,1)} %weight.1, bf16[512,512]{1,0:T(8,128)(2,1)} %targets.1), custom_call_target="tpu_custom_call" | custom-call | tf_op jit(solution)/shard_map/pallas_call | solution.py:365
  86.4 2.1 %shard_map.68 = (bf16[512,512]{1,0:T(8,128)(2,1)}, f32[128,512]{1,0:T(8,128)}, f32[2]{0:T(128)}) custom-call(bf16[512,512]{1,0:T(8,128)(2,1)} %get-tuple-element.6.ig, f32[128,512]{1,0:T(8,128)} %get-tuple-element.7.comb, f32[8,128]{1,0:T(8,128)} %get-tuple-element.8.norm, f32[128,512]{1,0:T(8,128)} %momentum.1), custom_call_target="tpu_custom_call" | custom-call | tf_op jit(solution)/shard_map/pallas_call | solution.py:414

commit v4 on v3

--- a/solution.py
+++ b/solution.py
@@ -54,7 +54,7 @@
     ig_out, comb_out, norm_out,
     ig, comb, norm, gacc,
     xin, w, tg, acc, gin, et, psend, precv, ppart, xrecv, gbuf, zsend, zrecv,
-    gsum, yred, tred, zred, mine,
+    gsum, red, zred, mine,
     ld_sem, out_sem, own_sem, iy_send, iy_recv, ix_send, ix_recv, is_send, is_recv,
     e_send, e_recv, p_send, p_recv, q_send, q_recv, z_send, z_recv, r_send, r_recv,
 ):
@@ -84,7 +84,12 @@
     tg_load.start()
 
     barrier = pltpu.get_barrier_semaphore()
-    peers = [at(dz=k) for k in range(1, NZ)] + [at(dy=k) for k in range(1, NY)] + [at(dt=k) for k in range(1, NT)]
+    line = [at(dz=k) for k in (4, 3, 5, 2, 6, 1, 7)]
+    plane = [
+        (z * NY + (y + dy) % NY, (x + dx) % NX * NC + (c + dc) % NC)
+        for dx in (2, 1, 3, 0) for dy in (2, 1, 3, 0) for dc in range(NC) if dx or dy or dc
+    ]
+    peers = line + plane
     for peer in peers:
         pl.semaphore_signal(barrier, inc=1, device_id=peer, device_id_type=MESH)
     pl.semaphore_wait(barrier, len(peers))
@@ -252,28 +257,28 @@
             gsum[p:p + 1, :] = jnp.sum(value, axis=0, keepdims=True)
         return lax.dot_general(
             ones, gsum[...], (((1,), (1,)), ((), ())), precision=lax.Precision.HIGHEST, preferred_element_type=F32
-        )
-
-    def reduce_stage(value, slot, buffer, count, me, peer_of):
+        )[0:1, :]
+
+    def reduce_stage(value, slot, buffer, me, peers_of):
         mine[slot] = value
         buffer[me] = value
-        for k in range(1, count):
-            remote(mine.at[slot], buffer.at[me], r_send.at[slot], r_recv.at[slot], peer_of(k)).start()
-        some = buffer.at[0:count - 1]
-        remote(some, some, r_send.at[slot], r_recv.at[slot], peer_of(1)).wait()
+        for peer in peers_of:
+            remote(mine.at[slot], buffer.at[me], r_send.at[slot], r_recv.at[slot], peer).start()
+        count = len(peers_of)
+        some = buffer.at[0:count]
+        remote(some, some, r_send.at[slot], r_recv.at[slot], peers_of[0]).wait()
         total = buffer[0]
-        for k in range(1, count):
+        for k in range(1, count + 1):
             total = total + buffer[k]
         return total
 
     def pick(vec, count):
         return [
-            jnp.sum(jnp.where(lane == p, vec, 0.0), axis=1, keepdims=True)[0:1, :] for p in range(count)
+            jnp.sum(jnp.where(lane[0:1] == p, vec, 0.0), axis=1, keepdims=True) for p in range(count)
         ]
 
     vec = to_lanes([gacc[a * NY + b] for a, b in YPAIRS])
-    vec = reduce_stage(vec, 0, yred.at[0], NY, y, lambda k: at(dy=k))
-    vec = reduce_stage(vec, 1, tred.at[0], NT, t, lambda k: at(dt=k))
+    vec = reduce_stage(vec, 0, red.at[0], y * NT + t, plane)
     weights, _, _ = tree(pick(vec, len(YPAIRS)), YPAIRS)
     weights = [v * (1.0 / math.sqrt(rows)) for v in weights]
 
@@ -327,9 +332,8 @@
         return tuple(out)
 
     vec = to_lanes(lax.fori_loop(0, cols // 16, z_step, (zero,) * len(ZPAIRS)))
-    vec = reduce_stage(vec, 2, zred, NZ, z, lambda k: at(dz=k))
-    vec = reduce_stage(vec, 3, yred.at[1], NY, y, lambda k: at(dy=k))
-    vec = reduce_stage(vec, 4, tred.at[1], NT, t, lambda k: at(dt=k))
+    vec = reduce_stage(vec, 1, zred, z, line)
+    vec = reduce_stage(vec, 2, red.at[1], y * NT + t, plane)
     weights, first_sq, second_sq = tree(pick(vec, len(ZPAIRS)), ZPAIRS)
     total = weights[0] * zrecv[0].astype(F32)
     for k in range(1, NZ):
@@ -337,7 +341,7 @@
     comb[...] = jnp.transpose(total)
     comb_copy = pltpu.make_async_copy(comb, comb_out, out_sem.at[1])
     comb_copy.start()
-    norm[...] = jnp.where(lane == 0, jnp.sqrt(first_sq), jnp.sqrt(second_sq)) * (1.0 / width)
+    norm[...] = jnp.where(lane[0:1] == 0, jnp.sqrt(first_sq), jnp.sqrt(second_sq)) * (1.0 / width)
     norm_copy = pltpu.make_async_copy(norm, norm_out, out_sem.at[2])
     norm_copy.start()
     for copy in z_copies:
@@ -367,14 +371,14 @@
         out_shape=(
             jax.ShapeDtypeStruct((cols, rows), BF16),
             jax.ShapeDtypeStruct((block, cols), F32),
-            jax.ShapeDtypeStruct((8, 128), F32),
+            jax.ShapeDtypeStruct((1, 128), F32),
         ),
         in_specs=[any_spec] * 3,
         out_specs=(any_spec,) * 3,
         scratch_shapes=[
             pltpu.VMEM((cols, rows), BF16),
             pltpu.VMEM((block, cols), F32),
-            pltpu.VMEM((8, 128), F32),
+            pltpu.VMEM((1, 128), F32),
             pltpu.VMEM((NY * NY, 8, 128), F32),
             pltpu.VMEM((rows, width), BF16),
             pltpu.VMEM((width, cols), BF16),
@@ -390,10 +394,9 @@
             pltpu.VMEM((NZ - 1, cols, block), BF16),
             pltpu.VMEM((NZ, cols, block), BF16),
             pltpu.VMEM((128, 128), F32),
-            pltpu.VMEM((2, NY, 8, 128), F32),
-            pltpu.VMEM((2, NT, 8, 128), F32),
-            pltpu.VMEM((NZ, 8, 128), F32),
-            pltpu.VMEM((5, 8, 128), F32),
+            pltpu.VMEM((2, NY * NT, 1, 128), F32),
+            pltpu.VMEM((NZ, 1, 128), F32),
+            pltpu.VMEM((3, 1, 128), F32),
             dma((2 * KCHUNKS + 1,)),
             dma((3,)),
             dma,
@@ -404,7 +407,7 @@
             dma((NX,)), dma((NX,)),
             dma((3,)), dma((3,)),
             dma((NZ - 1,)), dma((NZ - 1,)),
-            dma((5,)), dma((5,)),
+            dma((3,)), dma((3,)),
         ],
         compiler_params=pltpu.CompilerParams(
             collective_id=0, has_side_effects=True, vmem_limit_bytes=60 * 2**20

time: 88.6 us -> 84.2 us (0.950)
  Pallas kernels: 87.8 us -> 83.4 us
    pallas_call x1, Pallas kernels: 85.7 us -> 81.3 us  [body(): pl.pallas_call(kernel, out_shape=(jax.ShapeDtypeStruct((cols, rows), BF16...]
where the time goes in v4:
time: 84.2 us; the launch traced here: 84 us
  Pallas kernels  83.4 us (99%)
    pallas_call x1, Pallas kernels, body(): pl.pallas_call(kernel, out_shape=(jax.ShapeDtypeStruct((cols, rows), BF16...  81.3 us
    pallas_call x1, Pallas kernels, body(): pl.pallas_call(finish, out_shape=(jax.ShapeDtypeStruct((cols, rows), BF16...  2.12 us

profile of v4, /device:TPU:1, one launch (start us, length us, event | category | flops | bytes accessed | tf_op | source)
XLA Modules:
  0.0 84.0 jit_solution(522811197229040294)
XLA Ops:
  0.6 81.3 %shard_map.67 = (bf16[512,512]{1,0:T(8,128)(2,1)}, f32[128,512]{1,0:T(8,128)}, f32[1,128]{1,0:T(1,128)}) custom-call(bf16[512,4096]{1,0:T(8,128)(2,1)} %inputs.1, bf16[4096,512]{1,0:T(8,128)(2,1)} %weight.1, bf16[512,512]{1,0:T(8,128)(2,1)} %targets.1), custom_call_target="tpu_custom_call" | custom-call | tf_op jit(solution)/shard_map/pallas_call | solution.py:369
  81.9 2.1 %shard_map.68 = (bf16[512,512]{1,0:T(8,128)(2,1)}, f32[128,512]{1,0:T(8,128)}, f32[2]{0:T(128)}) custom-call(bf16[512,512]{1,0:T(8,128)(2,1)} %get-tuple-element.6.ig, f32[128,512]{1,0:T(8,128)} %get-tuple-element.7.comb, f32[1,128]{1,0:T(1,128)} %get-tuple-element.8.norm, f32[128,512]{1,0:T(8,128)} %momentum.1), custom_call_target="tpu_custom_call" | custom-call | tf_op jit(solution)/shard_map/pallas_call | solution.py:417

commit v5 on v4

--- a/solution.py
+++ b/solution.py
@@ -53,7 +53,7 @@
     inputs, weight, targets,
     ig_out, comb_out, norm_out,
     ig, comb, norm, gacc,
-    xin, w, tg, acc, gin, et, psend, precv, ppart, xrecv, gbuf, zsend, zrecv,
+    xin, w, tg, acc, gin, et, psend, precv, ppart, qin, xrecv, gbuf, zsend, zrecv,
     gsum, red, zred, mine,
     ld_sem, out_sem, own_sem, iy_send, iy_recv, ix_send, ix_recv, is_send, is_recv,
     e_send, e_recv, p_send, p_recv, q_send, q_recv, z_send, z_recv, r_send, r_recv,
@@ -299,21 +299,30 @@
     zrecv[z] = combine(z)
 
     q_copies = []
-    for j in (2, 1, 3):
-        copy = remote(ppart.at[j], xrecv.at[3 - j], q_send.at[j - 1], q_recv.at[3 - j], at_x(j, c))
+
+    def send_block(src, dst, sem, dx):
+        copy = remote(src, dst, q_send.at[sem], q_recv.at[sem], at_x(dx, c))
         copy.start()
         q_copies.append(copy)
+
+    send_block(ppart.at[2, low], qin.at[0], 0, 1)
+    send_block(ppart.at[2, high], qin.at[1], 1, 3)
+    send_block(ppart.at[1, high], xrecv.at[0, high], 2, 1)
+    send_block(ppart.at[3, low], xrecv.at[1, low], 3, 3)
     for k in (1, 2, 3):
         ref = gin.at[(y + k) % NY, my_rows]
         remote(ref, ref, iy_send.at[k - 1], iy_recv.at[k - 1], at(dy=k)).wait_send()
     for copy in e_copies + copies + p_copies:
         copy.wait_send()
-    for copy in q_copies:
+    q_copies[0].wait_recv()
+    ppart[1, 0:half] = (ppart[1, 0:half].astype(F32) + qin[0].astype(F32)).astype(BF16)
+    send_block(ppart.at[1, low], xrecv.at[0, low], 4, 1)
+    q_copies[1].wait_recv()
+    ppart[3, half:] = (ppart[3, half:].astype(F32) + qin[1].astype(F32)).astype(BF16)
+    send_block(ppart.at[3, high], xrecv.at[1, high], 5, 3)
+    for copy in q_copies[2:]:
         copy.wait_recv()
-    total = ppart[0].astype(F32)
-    for j in range(NX - 1):
-        total = total + xrecv[j].astype(F32)
-    ig[...] = total.astype(BF16)
+    ig[...] = (ppart[0].astype(F32) + (xrecv[0].astype(F32) + xrecv[1].astype(F32))).astype(BF16)
     ig_copy = pltpu.make_async_copy(ig, ig_out, out_sem.at[0])
     ig_copy.start()
     for copy in q_copies:
@@ -389,7 +398,8 @@
             pltpu.VMEM((NX, cols, rows), BF16),
             pltpu.VMEM((NX, cols, rows), BF16),
             pltpu.VMEM((NX, cols, rows), BF16),
-            pltpu.VMEM((NX - 1, cols, rows), BF16),
+            pltpu.VMEM((2, cols // 2, rows), BF16),
+            pltpu.VMEM((2, cols, rows), BF16),
             pltpu.VMEM((NY, cols, wide), F32),
             pltpu.VMEM((NZ - 1, cols, block), BF16),
             pltpu.VMEM((NZ, cols, block), BF16),
@@ -405,12 +415,12 @@
             dma((12,)), dma((12,)),
             dma((6,)), dma((6,)),
             dma((NX,)), dma((NX,)),
-            dma((3,)), dma((3,)),
+            dma((6,)), dma((6,)),
             dma((NZ - 1,)), dma((NZ - 1,)),
             dma((3,)), dma((3,)),
         ],
         compiler_params=pltpu.CompilerParams(
-            collective_id=0, has_side_effects=True, vmem_limit_bytes=60 * 2**20
+            collective_id=0, has_side_effects=True, vmem_limit_bytes=53 * 2**20
         ),
     )(inputs, weight, targets)
     smem = pl.BlockSpec(memory_space=pltpu.SMEM)
@@ -423,6 +433,7 @@
         ),
         in_specs=[vmem, vmem, smem, vmem],
         out_specs=(vmem, vmem, smem),
+        compiler_params=pltpu.CompilerParams(vmem_limit_bytes=4 * 2**20),
     )(summed, combined, norms, momentum)
 
 

time: 84.2 us -> 81.1 us (0.963)
  Pallas kernels: 83.4 us -> 80.4 us
    pallas_call x1, Pallas kernels: 81.3 us -> 78.9 us  [body(): pl.pallas_call(kernel, out_shape=(jax.ShapeDtypeStruct((cols, rows), BF16...]
where the time goes in v5:
time: 81.1 us; the launch traced here: 81 us
  Pallas kernels  80.4 us (99%)
    pallas_call x1, Pallas kernels, body(): pl.pallas_call(kernel, out_shape=(jax.ShapeDtypeStruct((cols, rows), BF16...  78.9 us

profile of v5, /device:TPU:1, one launch (start us, length us, event | category | flops | bytes accessed | tf_op | source)
XLA Modules:
  0.0 81.0 jit_solution(16814600576287025954)
XLA Ops:
  0.6 0.0 copy-start
  0.6 78.9 %shard_map.67 = (bf16[512,512]{1,0:T(8,128)(2,1)S(1)}, f32[128,512]{1,0:T(8,128)S(1)}, f32[1,128]{1,0:T(1,128)S(1)}) custom-call(bf16[512,4096]{1,0:T(8,128)(2,1)} %inputs.1, bf16[4096,512]{1,0:T(8,128)(2,1)} %weight.1, bf16[512,512]{1,0:T(8,128)(2,1)} %targets.1), custom_call_target="tpu_custom_call" | custom-call | tf_op jit(solution)/shard_map/pallas_call | solution.py:378
  79.5 0.0 copy-done
  79.6 1.5 %shard_map.68 = (bf16[512,512]{1,0:T(8,128)(2,1)}, f32[128,512]{1,0:T(8,128)}, f32[2]{0:T(128)}) custom-call(bf16[512,512]{1,0:T(8,128)(2,1)S(1)} %get-tuple-element.6.ig, f32[128,512]{1,0:T(8,128)S(1)} %get-tuple-element.7.comb, f32[1,128]{1,0:T(1,128)S(1)} %get-tuple-element.8.norm, f32[128,512]{1,0:T(8,128)S(1)} %copy-done), custom_call_target="tpu_custom_call" | custom-call | tf_op jit(solution)/shard_map/pallas_call | solution.py:427
Async XLA Ops:
  0.6 78.9 %copy-start = (f32[128,512]{1,0:T(8,128)S(1)}, f32[128,512]{1,0:T(8,128)}, u32[]{:S(2)}) copy-start(f32[128,512]{1,0:T(8,128)} %momentum.1) | copy-start | bytes 786436

commit v6 on v5

--- a/solution.py
+++ b/solution.py
@@ -52,7 +52,7 @@
 def kernel(
     inputs, weight, targets,
     ig_out, comb_out, norm_out,
-    ig, comb, norm, gacc,
+    ig, comb, norm, gacc, zacc,
     xin, w, tg, acc, gin, et, psend, precv, ppart, qin, xrecv, gbuf, zsend, zrecv,
     gsum, red, zred, mine,
     ld_sem, out_sem, own_sem, iy_send, iy_recv, ix_send, ix_recv, is_send, is_recv,
@@ -73,6 +73,15 @@
     def at_x(dx, core):
         return (dp, (x + dx) % NX * NC + core)
 
+    barrier = pltpu.get_barrier_semaphore()
+    line = [at(dz=k) for k in (4, 3, 5, 2, 6, 1, 7)]
+    plane = [
+        (z * NY + (y + dy) % NY, (x + dx) % NX * NC + (c + dc) % NC)
+        for dx in (2, 1, 3, 0) for dy in (2, 1, 3, 0) for dc in range(NC) if dx or dy or dc
+    ]
+    peers = line + plane
+    for peer in peers:
+        pl.semaphore_signal(barrier, inc=1, device_id=peer, device_id_type=MESH)
     loads = []
     for i in range(KCHUNKS):
         a = pltpu.make_async_copy(inputs.at[:, i * kc:(i + 1) * kc], xin.at[:, i * kc:(i + 1) * kc], ld_sem.at[2 * i])
@@ -83,15 +92,6 @@
     tg_load = pltpu.make_async_copy(targets, tg, ld_sem.at[2 * KCHUNKS])
     tg_load.start()
 
-    barrier = pltpu.get_barrier_semaphore()
-    line = [at(dz=k) for k in (4, 3, 5, 2, 6, 1, 7)]
-    plane = [
-        (z * NY + (y + dy) % NY, (x + dx) % NX * NC + (c + dc) % NC)
-        for dx in (2, 1, 3, 0) for dy in (2, 1, 3, 0) for dc in range(NC) if dx or dy or dc
-    ]
-    peers = line + plane
-    for peer in peers:
-        pl.semaphore_signal(barrier, inc=1, device_id=peer, device_id_type=MESH)
     pl.semaphore_wait(barrier, len(peers))
 
     def remote(src, dst, send, recv, peer):
@@ -230,7 +230,7 @@
             values = [gbuf[k, at_rows, :] for k in items]
             return tuple(s + fold(values[a] * values[b]) for s, (a, b) in zip(sums, pairs))
 
-        sums = lax.fori_loop(0, cols // 8, step, (zero,) * len(pairs))
+        sums = lax.fori_loop(0, cols // 8, step, (zero,) * len(pairs), unroll=4)
         for value, (a, b) in zip(sums, pairs):
             low_index, high_index = jnp.minimum(items[a], items[b]), jnp.maximum(items[a], items[b])
             gacc[low_index * NY + high_index] = value
@@ -328,36 +328,45 @@
     for copy in q_copies:
         copy.wait_send()
 
-    for k in range(1, NZ):
-        remote(zrecv.at[(z + k) % NZ], zrecv.at[(z + k) % NZ], z_send.at[k - 1], z_recv.at[k - 1], at(dz=1)).wait_recv()
-
-    def z_step(i, sums):
-        at_rows = pl.ds(pl.multiple_of(i * 16, 16), 16)
-        items = [zrecv[k, at_rows, :].astype(F32) for k in range(NZ)]
-        out = []
-        for s, (a, b) in zip(sums, ZPAIRS):
-            product = items[a] * items[b]
-            out.append(s + product[0:8] + product[8:16])
-        return tuple(out)
-
-    vec = to_lanes(lax.fori_loop(0, cols // 16, z_step, (zero,) * len(ZPAIRS)))
+    def z_wait(k):
+        ref = zrecv.at[(z + k) % NZ]
+        remote(ref, ref, z_send.at[k - 1], z_recv.at[k - 1], at(dz=1)).wait_recv()
+
+    def z_products(items, pairs):
+        def step(i, sums):
+            at_rows = pl.ds(pl.multiple_of(i * 16, 16), 16)
+            values = [zrecv[k, at_rows, :].astype(F32) for k in items]
+            out = []
+            for s, (a, b) in zip(sums, pairs):
+                product = values[a] * values[b]
+                out.append(s + (product[0:8] + product[8:16]))
+            return tuple(out)
+
+        sums = lax.fori_loop(0, cols // 16, step, (zero,) * len(pairs), unroll=2)
+        for value, (a, b) in zip(sums, pairs):
+            low_index, high_index = jnp.minimum(items[a], items[b]), jnp.maximum(items[a], items[b])
+            zacc[low_index * NZ + high_index] = value
+
+    late, early = (7, 1), (4, 3, 5, 2, 6)
+    for k in early:
+        z_wait(k)
+    items = [(z + k) % NZ for k in late + early + (0,)]
+    z_products(items[2:], [(a, b) for a in range(6) for b in range(a, 6)])
+    for k in late:
+        z_wait(k)
+    z_products(items, [(a, b) for a in range(2) for b in range(a, NZ)])
+    vec = to_lanes([zacc[a * NZ + b] for a, b in ZPAIRS])
     vec = reduce_stage(vec, 1, zred, z, line)
     vec = reduce_stage(vec, 2, red.at[1], y * NT + t, plane)
     weights, first_sq, second_sq = tree(pick(vec, len(ZPAIRS)), ZPAIRS)
     total = weights[0] * zrecv[0].astype(F32)
     for k in range(1, NZ):
         total = total + weights[k] * zrecv[k].astype(F32)
-    comb[...] = jnp.transpose(total)
-    comb_copy = pltpu.make_async_copy(comb, comb_out, out_sem.at[1])
-    comb_copy.start()
-    norm[...] = jnp.where(lane[0:1] == 0, jnp.sqrt(first_sq), jnp.sqrt(second_sq)) * (1.0 / width)
-    norm_copy = pltpu.make_async_copy(norm, norm_out, out_sem.at[2])
-    norm_copy.start()
+    comb_out[...] = jnp.transpose(total)
+    norm_out[...] = jnp.where(lane[0:1] == 0, jnp.sqrt(first_sq), jnp.sqrt(second_sq)) * (1.0 / width)
     for copy in z_copies:
         copy.wait_send()
     ig_copy.wait()
-    comb_copy.wait()
-    norm_copy.wait()
 
 
 def finish(ig, comb, norm, momentum, ig_out, momentum_out, norm_out):
@@ -383,12 +392,13 @@
             jax.ShapeDtypeStruct((1, 128), F32),
         ),
         in_specs=[any_spec] * 3,
-        out_specs=(any_spec,) * 3,
+        out_specs=(any_spec, vmem, vmem),
         scratch_shapes=[
             pltpu.VMEM((cols, rows), BF16),
             pltpu.VMEM((block, cols), F32),
             pltpu.VMEM((1, 128), F32),
             pltpu.VMEM((NY * NY, 8, 128), F32),
+            pltpu.VMEM((NZ * NZ, 8, 128), F32),
             pltpu.VMEM((rows, width), BF16),
             pltpu.VMEM((width, cols), BF16),
             pltpu.VMEM((rows, cols), BF16),

time: 81.1 us -> 80.2 us (0.989)
  Pallas kernels: 80.4 us -> 79.5 us
    pallas_call x1, Pallas kernels: 78.9 us -> 78 us  [body(): pl.pallas_call(kernel, out_shape=(jax.ShapeDtypeStruct((cols, rows), BF16...]
where the time goes in v6:
time: 80.2 us; the launch traced here: 80.1 us
  Pallas kernels  79.5 us (99%)
    pallas_call x1, Pallas kernels, body(): pl.pallas_call(kernel, out_shape=(jax.ShapeDtypeStruct((cols, rows), BF16...  78 us

profile of v6, /device:TPU:1, one launch (start us, length us, event | category | flops | bytes accessed | tf_op | source)
XLA Modules:
  0.0 80.1 jit_solution(13104138957857148895)
XLA Ops:
  0.6 0.0 copy-start
  0.6 78.0 %shard_map.67 = (bf16[512,512]{1,0:T(8,128)(2,1)S(1)}, f32[128,512]{1,0:T(8,128)S(1)}, f32[1,128]{1,0:T(1,128)S(1)}) custom-call(bf16[512,4096]{1,0:T(8,128)(2,1)} %inputs.1, bf16[4096,512]{1,0:T(8,128)(2,1)} %weight.1, bf16[512,512]{1,0:T(8,128)(2,1)} %targets.1), custom_call_target="tpu_custom_call" | custom-call | tf_op jit(solution)/shard_map/pallas_call | solution.py:387
  78.6 0.0 copy-done
  78.6 1.5 %shard_map.68 = (bf16[512,512]{1,0:T(8,128)(2,1)}, f32[128,512]{1,0:T(8,128)}, f32[2]{0:T(128)}) custom-call(bf16[512,512]{1,0:T(8,128)(2,1)S(1)} %get-tuple-element.6.ig, f32[128,512]{1,0:T(8,128)S(1)} %get-tuple-element.7.comb, f32[1,128]{1,0:T(1,128)S(1)} %get-tuple-element.8.norm, f32[128,512]{1,0:T(8,128)S(1)} %copy-done), custom_call_target="tpu_custom_call" | custom-call | tf_op jit(solution)/shard_map/pallas_call | solution.py:437
Async XLA Ops:
  0.6 78.0 %copy-start = (f32[128,512]{1,0:T(8,128)S(1)}, f32[128,512]{1,0:T(8,128)}, u32[]{:S(2)}) copy-start(f32[128,512]{1,0:T(8,128)} %momentum.1) | copy-start | bytes 786436

commit v7 on v6

--- a/solution.py
+++ b/solution.py
@@ -372,8 +372,7 @@
 def finish(ig, comb, norm, momentum, ig_out, momentum_out, norm_out):
     ig_out[...] = ig[...]
     momentum_out[...] = 0.9 * momentum[...] + comb[...]
-    norm_out[0] = norm[0, 0]
-    norm_out[1] = norm[0, 1]
+    norm_out[...] = norm[0, 0:2]
 
 
 def body(inputs, weight, targets, momentum):
@@ -433,7 +432,6 @@
             collective_id=0, has_side_effects=True, vmem_limit_bytes=53 * 2**20
         ),
     )(inputs, weight, targets)
-    smem = pl.BlockSpec(memory_space=pltpu.SMEM)
     return pl.pallas_call(
         finish,
         out_shape=(
@@ -441,8 +439,8 @@
             jax.ShapeDtypeStruct((block, cols), F32),
             jax.ShapeDtypeStruct((2,), F32),
         ),
-        in_specs=[vmem, vmem, smem, vmem],
-        out_specs=(vmem, vmem, smem),
+        in_specs=[vmem, vmem, vmem, vmem],
+        out_specs=(vmem, vmem, vmem),
         compiler_params=pltpu.CompilerParams(vmem_limit_bytes=4 * 2**20),
     )(summed, combined, norms, momentum)
 

time: 80.2 us -> 79.7 us (level)
  no operation moved by 1% of the time
where the time goes in v7:
time: 79.7 us; the launch traced here: 79.6 us
  Pallas kernels  78.9 us (99%)
    pallas_call x1, Pallas kernels, body(): pl.pallas_call(kernel, out_shape=(jax.ShapeDtypeStruct((cols, rows), BF16...  78 us

profile of v7, /device:TPU:1, one launch (start us, length us, event | category | flops | bytes accessed | tf_op | source)
XLA Modules:
  0.0 79.6 jit_solution(11452324839935609457)
XLA Ops:
  0.6 0.0 copy-start
  0.6 78.0 %shard_map.67 = (bf16[512,512]{1,0:T(8,128)(2,1)S(1)}, f32[128,512]{1,0:T(8,128)S(1)}, f32[1,128]{1,0:T(1,128)S(1)}) custom-call(bf16[512,4096]{1,0:T(8,128)(2,1)} %inputs.1, bf16[4096,512]{1,0:T(8,128)(2,1)} %weight.1, bf16[512,512]{1,0:T(8,128)(2,1)} %targets.1), custom_call_target="tpu_custom_call" | custom-call | tf_op jit(solution)/shard_map/pallas_call | solution.py:386
  78.6 0.0 copy-done
  78.6 0.9 %shard_map.68 = (bf16[512,512]{1,0:T(8,128)(2,1)}, f32[128,512]{1,0:T(8,128)}, f32[2]{0:T(128)}) custom-call(bf16[512,512]{1,0:T(8,128)(2,1)S(1)} %get-tuple-element.6.ig, f32[128,512]{1,0:T(8,128)S(1)} %get-tuple-element.7.comb, f32[1,128]{1,0:T(1,128)S(1)} %get-tuple-element.8.norm, f32[128,512]{1,0:T(8,128)S(1)} %copy-done), custom_call_target="tpu_custom_call" | custom-call | tf_op jit(solution)/shard_map/pallas_call | solution.py:435
Async XLA Ops:
  0.6 78.0 %copy-start = (f32[128,512]{1,0:T(8,128)S(1)}, f32[128,512]{1,0:T(8,128)}, u32[]{:S(2)}) copy-start(f32[128,512]{1,0:T(8,128)} %momentum.1) | copy-start | bytes 786436

commit v8 on v7

--- a/solution.py
+++ b/solution.py
@@ -342,7 +342,7 @@
                 out.append(s + (product[0:8] + product[8:16]))
             return tuple(out)
 
-        sums = lax.fori_loop(0, cols // 16, step, (zero,) * len(pairs), unroll=2)
+        sums = lax.fori_loop(0, cols // 16, step, (zero,) * len(pairs), unroll=4)
         for value, (a, b) in zip(sums, pairs):
             low_index, high_index = jnp.minimum(items[a], items[b]), jnp.maximum(items[a], items[b])
             zacc[low_index * NZ + high_index] = value

time: 79.7 us -> 79.6 us (level)
  no operation moved by 1% of the time
where the time goes in v8:
time: 79.6 us; the launch traced here: 79.5 us
  Pallas kernels  78.8 us (99%)
    pallas_call x1, Pallas kernels, body(): pl.pallas_call(kernel, out_shape=(jax.ShapeDtypeStruct((cols, rows), BF16...  77.9 us

profile of v8, /device:TPU:1, one launch (start us, length us, event | category | flops | bytes accessed | tf_op | source)
XLA Modules:
  0.0 79.5 jit_solution(10310834034730053890)
XLA Ops:
  0.6 0.0 copy-start
  0.6 77.9 %shard_map.67 = (bf16[512,512]{1,0:T(8,128)(2,1)S(1)}, f32[128,512]{1,0:T(8,128)S(1)}, f32[1,128]{1,0:T(1,128)S(1)}) custom-call(bf16[512,4096]{1,0:T(8,128)(2,1)} %inputs.1, bf16[4096,512]{1,0:T(8,128)(2,1)} %weight.1, bf16[512,512]{1,0:T(8,128)(2,1)} %targets.1), custom_call_target="tpu_custom_call" | custom-call | tf_op jit(solution)/shard_map/pallas_call | solution.py:386
  78.5 0.0 copy-done
  78.6 0.9 %shard_map.68 = (bf16[512,512]{1,0:T(8,128)(2,1)}, f32[128,512]{1,0:T(8,128)}, f32[2]{0:T(128)}) custom-call(bf16[512,512]{1,0:T(8,128)(2,1)S(1)} %get-tuple-element.6.ig, f32[128,512]{1,0:T(8,128)S(1)} %get-tuple-element.7.comb, f32[1,128]{1,0:T(1,128)S(1)} %get-tuple-element.8.norm, f32[128,512]{1,0:T(8,128)S(1)} %copy-done), custom_call_target="tpu_custom_call" | custom-call | tf_op jit(solution)/shard_map/pallas_call | solution.py:435
Async XLA Ops:
  0.6 77.9 %copy-start = (f32[128,512]{1,0:T(8,128)S(1)}, f32[128,512]{1,0:T(8,128)}, u32[]{:S(2)}) copy-start(f32[128,512]{1,0:T(8,128)} %momentum.1) | copy-start | bytes 786436
